TPU v7x, 128 devices: a whole 4x4x4 slice. The times are simulated.
128 devices in a mesh: dom: 16 (over y_lo, z, core), rep: 8 (over y_hi, x).
Axes of the slice: x: 4, y: 4 (y_hi: 2, y_lo: 2; y = y_hi * 2 + y_lo), z: 4, core: 2. Of those that a mesh axis runs over, the one named last changes fastest.
Arguments:
- node_features: bfloat16 [65536, 256], P(('dom', 'rep')), may hold values from -6 to 6
- weight: bfloat16 [256, 256], replicated, may hold values from -0.375 to 0.375
- cotangent: bfloat16 [65536, 256], P(('dom', 'rep')), may hold values from -6 to 6
- tile_row: int32 [16, 8, 512], P('dom', 'rep'), may hold values from 0 to 31
- tile_col: int32 [16, 8, 512], P('dom', 'rep'), may hold values from 0 to 63
- tile_values: bfloat16 [16, 8, 512, 128, 128], P('dom', 'rep'), may hold values from -0.0625 to 0.0625
- tile_count: int32 [16, 8], P('dom', 'rep'), may hold values from 128 to 512, as said below
Outputs:
- output: bfloat16 [65536, 256], P(('dom', 'rep'))
- grad_features: bfloat16 [65536, 256], P(('dom', 'rep'))
- grad_weight: float32 [256, 256], replicated
Inputs may be any that keep to these rules, and one draw needn't show every extreme that they name: Live slots are the first tile_count slots of each device's list; some device has all 512 slots live.
All inputs are finite; a program needn't handle non-finite values.
Results may differ from a plain program's by a relative error of at most 0.0061.
Values may be sent and summed in bfloat16 or wider, within the bound.
No kernel may reach another device: no remote copies, remote signals or barrier semaphores. Data moves between devices by JAX's collectives and lax.ppermute only.
A program may use at most 192 MiB of HBM per device.

v0:
```python
import jax
import jax.numpy as jnp
from jax import lax
from jax.sharding import PartitionSpec as P


def silu_slope(summed):
    sig = jax.nn.sigmoid(summed)
    return sig * (1.0 + summed * (1.0 - sig))


def tile_products(values, pick_index, place_index, active, source, out_blocks, flipped):
    slots = values.shape[0]
    feature_width = source.shape[2]
    per_turn = min(slots, 128)
    pattern = "tba,tbf->taf" if flipped else "tab,tbf->taf"

    def accumulate(turn_index, summed):
        first_slot = turn_index * per_turn
        block_values = lax.dynamic_slice_in_dim(values, first_slot, per_turn, 0)
        picks = lax.dynamic_slice_in_dim(pick_index, first_slot, per_turn, 0)
        picked = jnp.take(source, picks, axis=0)
        products = jnp.einsum(pattern, block_values, picked, preferred_element_type=jnp.float32)
        places = lax.dynamic_slice_in_dim(place_index, first_slot, per_turn, 0)
        enabled = lax.dynamic_slice_in_dim(active, first_slot, per_turn, 0)
        products = products * enabled.astype(jnp.float32)[:, None, None]
        return summed.at[places].add(products)

    initial = jnp.zeros((out_blocks, 128, feature_width), jnp.float32)
    summed = lax.fori_loop(0, slots // per_turn, accumulate, initial)
    return summed.reshape(out_blocks * 128, feature_width)


def body(node_features, weight, cotangent, tile_row, tile_col, tile_values, tile_count):
    rows_here = node_features.shape[0]
    feature_width = weight.shape[0]
    dom_size = lax.axis_size("dom")
    rep_size = lax.axis_size("rep")
    slots = tile_row.shape[2]
    row_index = tile_row.reshape(slots)
    col_index = tile_col.reshape(slots)
    values = tile_values.reshape(slots, 128, 128)
    active = lax.broadcasted_iota(jnp.int32, (slots,), 0) < tile_count.reshape(())
    projected = jnp.dot(node_features, weight, preferred_element_type=jnp.float32).astype(
        jnp.bfloat16
    )
    gathered = lax.all_gather(projected, "dom", axis=0, tiled=True)
    source = gathered.reshape(-1, 128, feature_width)
    part_blocks = rep_size * rows_here // 128
    partial_value = tile_products(values, col_index, row_index, active, source, part_blocks, False)
    summed = lax.psum_scatter(partial_value, "rep", scatter_dimension=0, tiled=True)
    output = jax.nn.silu(summed).astype(jnp.bfloat16)
    grad_own = (cotangent.astype(jnp.float32) * silu_slope(summed)).astype(jnp.bfloat16)
    grad_block = lax.all_gather(grad_own, "rep", axis=0, tiled=True)
    back_blocks = dom_size * rows_here // 128
    back_partial = tile_products(
        values,
        row_index,
        col_index,
        active,
        grad_block.reshape(-1, 128, feature_width),
        back_blocks,
        True,
    )
    grad_projected = lax.psum_scatter(back_partial, "dom", scatter_dimension=0, tiled=True).astype(
        jnp.bfloat16
    )
    grad_features = jnp.dot(grad_projected, weight.T, preferred_element_type=jnp.float32).astype(
        jnp.bfloat16
    )
    local_weight = jnp.dot(node_features.T, grad_projected, preferred_element_type=jnp.float32)
    grad_weight = lax.psum(local_weight, ("dom", "rep"))
    return (output, grad_features, grad_weight)


def solution(mesh):
    placed = (
        P(("dom", "rep"), None),
        P(),
        P(("dom", "rep"), None),
        P("dom", "rep", None),
        P("dom", "rep", None),
        P("dom", "rep", None, None, None),
        P("dom", "rep"),
    )
    return jax.shard_map(
        body,
        mesh=mesh,
        in_specs=placed,
        out_specs=(P(("dom", "rep"), None), P(("dom", "rep"), None), P()),
        check_vma=False,
    )
```

profile of v0, /device:TPU:1, one launch (start us, length us, event | category | flops | bytes accessed | tf_op | source)
XLA Modules:
  0.0 908.0 jit_solution(10777865380881318707)
XLA Ops:
  7.2 0.0 all-gather.3.cloned.1.call-start
  7.2 0.9 copy-done
  8.1 1.8 convolution_convert_fusion.1
  10.0 0.0 reduce-scatter.3.cloned.1.call-start
  10.7 40.7 %all-gather.3.cloned.1.call-done = bf16[8192,256]{1,0:T(8,128)(2,1)} async-done(((bf16[512,256]{1,0:T(8,128)(2,1)}), bf16[8192,256]{1,0:T(8,128)(2,1)}) %all-gather.3.cloned.1.call-update) | async-done | bytes 4194320 | tf_op jit(solution)/shard_map/all_gather | solution.py:47
  51.4 2.4 broadcast_in_dim.74
  53.8 244.2 %while.26 = (s32[]{:T(128)}, f32[32,128,256]{2,1,0:T(8,128)}, s32[512]{0:T(512)}, bf16[512,128,128]{2,1,0:T(8,128)(2,1)}, s32[512]{0:T(512)}, /*index=5*/bf16[64...) while((s32[]{:T(128)}, f32[32,128,256]{2,1,0:T(8,128)}, ...), condition=%wide.region_2.3_spmd, body=%wide.region_0.2_spmd.sunk | while | flops 1086327040 | bytes 96478248 | solution.py:30
  53.8 0.8 compare_and_fusion.4
  54.6 8.8 gather_fusion
  63.4 12.8 %convolution_multiply_fusion.4 = f32[128,128,256]{2,1,0:T(8,128)} fusion(f32[128]{0:T(128)S(1)} %get-tuple-element.384, bf16[128,128,256]{2,1,0:T(8,128)(2,1)} %gather_fusion, pred[128]{0:T(512)(128)(4,1)S(1)} %get-tuple-element.386, bf16[512,128,128]{2,1,0:T(8,128)(2,1)} %get-tuple-element.422, s32[]{:T(128)S(6)} %select_n.85), kind=kOutput, calls=%fused_computation.4.clone.1 | convolution fusion | flops 1082130432 | bytes 29360772 | tf_op jit(solution)/shard_map/while/body/eval_jaxpr/tab,tbf->taf/dot_general | solution.py:23
  76.2 0.8 compare_select_fusion.8
  76.9 38.1 %scatter_fusion = f32[32,128,256]{2,1,0:T(8,128)} fusion(f32[32,128,256]{2,1,0:T(8,128)} %get-tuple-element.409, s32[128]{0:T(128)S(1)} %compare_select_fusion.8, f32[128,128,256]{2,1,0:T(8,128)} %convolution_multiply_fusion.4), kind=kCustom, calls=%fused_computation.2.clone.1 | custom fusion | flops 4194304 | bytes 50332160 | tf_op jit(solution)/shard_map/while/body/eval_jaxpr/scatter-add | solution.py:27
  115.0 0.8 compare_and_fusion.4
  115.8 8.8 gather_fusion
  124.5 12.8 %convolution_multiply_fusion.4 = f32[128,128,256]{2,1,0:T(8,128)} fusion(f32[128]{0:T(128)S(1)} %get-tuple-element.384, bf16[128,128,256]{2,1,0:T(8,128)(2,1)} %gather_fusion, pred[128]{0:T(512)(128)(4,1)S(1)} %get-tuple-element.386, bf16[512,128,128]{2,1,0:T(8,128)(2,1)} %get-tuple-element.422, s32[]{:T(128)S(6)} %select_n.85), kind=kOutput, calls=%fused_computation.4.clone.1 | convolution fusion | flops 1082130432 | bytes 29360772 | tf_op jit(solution)/shard_map/while/body/eval_jaxpr/tab,tbf->taf/dot_general | solution.py:23
  137.3 0.8 compare_select_fusion.8
  138.1 38.1 %scatter_fusion = f32[32,128,256]{2,1,0:T(8,128)} fusion(f32[32,128,256]{2,1,0:T(8,128)} %get-tuple-element.409, s32[128]{0:T(128)S(1)} %compare_select_fusion.8, f32[128,128,256]{2,1,0:T(8,128)} %convolution_multiply_fusion.4), kind=kCustom, calls=%fused_computation.2.clone.1 | custom fusion | flops 4194304 | bytes 50332160 | tf_op jit(solution)/shard_map/while/body/eval_jaxpr/scatter-add | solution.py:27
  176.2 0.8 compare_and_fusion.4
  176.9 8.8 gather_fusion
  185.7 12.8 %convolution_multiply_fusion.4 = f32[128,128,256]{2,1,0:T(8,128)} fusion(f32[128]{0:T(128)S(1)} %get-tuple-element.384, bf16[128,128,256]{2,1,0:T(8,128)(2,1)} %gather_fusion, pred[128]{0:T(512)(128)(4,1)S(1)} %get-tuple-element.386, bf16[512,128,128]{2,1,0:T(8,128)(2,1)} %get-tuple-element.422, s32[]{:T(128)S(6)} %select_n.85), kind=kOutput, calls=%fused_computation.4.clone.1 | convolution fusion | flops 1082130432 | bytes 29360772 | tf_op jit(solution)/shard_map/while/body/eval_jaxpr/tab,tbf->taf/dot_general | solution.py:23
  198.5 0.8 compare_select_fusion.8
  199.3 37.7 %scatter_fusion = f32[32,128,256]{2,1,0:T(8,128)} fusion(f32[32,128,256]{2,1,0:T(8,128)} %get-tuple-element.409, s32[128]{0:T(128)S(1)} %compare_select_fusion.8, f32[128,128,256]{2,1,0:T(8,128)} %convolution_multiply_fusion.4), kind=kCustom, calls=%fused_computation.2.clone.1 | custom fusion | flops 4194304 | bytes 50332160 | tf_op jit(solution)/shard_map/while/body/eval_jaxpr/scatter-add | solution.py:27
  237.0 0.8 compare_and_fusion.4
  237.7 8.8 gather_fusion
  246.5 12.8 %convolution_multiply_fusion.4 = f32[128,128,256]{2,1,0:T(8,128)} fusion(f32[128]{0:T(128)S(1)} %get-tuple-element.384, bf16[128,128,256]{2,1,0:T(8,128)(2,1)} %gather_fusion, pred[128]{0:T(512)(128)(4,1)S(1)} %get-tuple-element.386, bf16[512,128,128]{2,1,0:T(8,128)(2,1)} %get-tuple-element.422, s32[]{:T(128)S(6)} %select_n.85), kind=kOutput, calls=%fused_computation.4.clone.1 | convolution fusion | flops 1082130432 | bytes 29360772 | tf_op jit(solution)/shard_map/while/body/eval_jaxpr/tab,tbf->taf/dot_general | solution.py:23
  259.3 0.8 compare_select_fusion.8
  260.1 37.9 %scatter_fusion = f32[32,128,256]{2,1,0:T(8,128)} fusion(f32[32,128,256]{2,1,0:T(8,128)} %get-tuple-element.409, s32[128]{0:T(128)S(1)} %compare_select_fusion.8, f32[128,128,256]{2,1,0:T(8,128)} %convolution_multiply_fusion.4), kind=kCustom, calls=%fused_computation.2.clone.1 | custom fusion | flops 4194304 | bytes 50332160 | tf_op jit(solution)/shard_map/while/body/eval_jaxpr/scatter-add | solution.py:27
  298.0 0.0 reduce-scatter.3.cloned.1.call-update
  298.0 0.0 all-gather.5.cloned.1.call-start
  298.0 83.2 %reduce-scatter.3.cloned.1.call-done = f32[512,256]{1,0:T(8,128)} async-done(((f32[4096,256]{1,0:T(8,128)}), f32[512,256]{1,0:T(8,128)}) %reduce-scatter.3.cloned.1.call-update) | async-done | bytes 524304 | tf_op jit(solution)/shard_map/reduce_scatter | solution.py:51
  381.3 2.1 multiply_convert_fusion
  383.4 0.0 all-gather.5.cloned.1.call-update
  383.4 0.2 reduce-scatter.5.cloned.1.call-start
  383.6 22.4 %copy.10 = bf16[1,1,512,128,128]{3,4,2,1,0:T(8,128)(2,1)} copy(bf16[1,1,512,128,128]{4,3,2,1,0:T(8,128)(2,1)} %bitcast.21) | data formatting | bytes 33554432 | tf_op args[5]
  406.0 31.9 %all-gather.5.cloned.1.call-done = bf16[4096,256]{1,0:T(8,128)(2,1)} async-done(((bf16[512,256]{1,0:T(8,128)(2,1)}), bf16[4096,256]{1,0:T(8,128)(2,1)}) %all-gather.5.cloned.1.call-update) | async-done | bytes 2097168 | tf_op jit(solution)/shard_map/all_gather | solution.py:54
  437.9 4.2 broadcast_in_dim.75
  442.1 236.8 %while.27 = (s32[]{:T(128)}, f32[64,128,256]{2,1,0:T(8,128)}, s32[512]{0:T(512)}, bf16[512,128,128]{1,2,0:T(8,128)(2,1)}, s32[512]{0:T(512)}, /*index=5*/bf16[32...) while((s32[]{:T(128)}, f32[64,128,256]{2,1,0:T(8,128)}, ...), condition=%wide.region_6.7_spmd, body=%wide.region_4.6_spmd.sunk | while | flops 1086327040 | bytes 96478248 | solution.py:30
  442.1 0.8 compare_and_fusion.5
  442.9 6.6 gather_fusion.1
  449.5 12.8 %convolution_multiply_fusion.5 = f32[128,128,256]{2,1,0:T(8,128)} fusion(f32[128]{0:T(128)S(1)} %get-tuple-element.394, bf16[128,128,256]{2,1,0:T(8,128)(2,1)} %gather_fusion.1, pred[128]{0:T(512)(128)(4,1)S(1)} %get-tuple-element.396, bf16[512,128,128]{1,2,0:T(8,128)(2,1)} %get-tuple-element.455, s32[]{:T(128)S(6)} %select_n.88), kind=kOutput, calls=%fused_computation.16.clone.1 | convolution fusion | flops 1082130432 | bytes 29360772 | tf_op jit(solution)/shard_map/while/body/eval_jaxpr/tba,tbf->taf/dot_general | solution.py:23
  462.3 0.8 compare_select_fusion.9
  463.1 38.5 %scatter_fusion.1 = f32[64,128,256]{2,1,0:T(8,128)} fusion(f32[64,128,256]{2,1,0:T(8,128)} %get-tuple-element.442, s32[128]{0:T(128)S(1)} %compare_select_fusion.9, f32[128,128,256]{2,1,0:T(8,128)} %convolution_multiply_fusion.5), kind=kCustom, calls=%fused_computation.3.clone.1 | custom fusion | flops 4194304 | bytes 50332160 | tf_op jit(solution)/shard_map/while/body/eval_jaxpr/scatter-add | solution.py:27
  501.6 0.8 compare_and_fusion.5
  502.3 6.6 gather_fusion.1
  508.9 12.8 %convolution_multiply_fusion.5 = f32[128,128,256]{2,1,0:T(8,128)} fusion(f32[128]{0:T(128)S(1)} %get-tuple-element.394, bf16[128,128,256]{2,1,0:T(8,128)(2,1)} %gather_fusion.1, pred[128]{0:T(512)(128)(4,1)S(1)} %get-tuple-element.396, bf16[512,128,128]{1,2,0:T(8,128)(2,1)} %get-tuple-element.455, s32[]{:T(128)S(6)} %select_n.88), kind=kOutput, calls=%fused_computation.16.clone.1 | convolution fusion | flops 1082130432 | bytes 29360772 | tf_op jit(solution)/shard_map/while/body/eval_jaxpr/tba,tbf->taf/dot_general | solution.py:23
  521.7 0.8 compare_select_fusion.9
  522.5 38.1 %scatter_fusion.1 = f32[64,128,256]{2,1,0:T(8,128)} fusion(f32[64,128,256]{2,1,0:T(8,128)} %get-tuple-element.442, s32[128]{0:T(128)S(1)} %compare_select_fusion.9, f32[128,128,256]{2,1,0:T(8,128)} %convolution_multiply_fusion.5), kind=kCustom, calls=%fused_computation.3.clone.1 | custom fusion | flops 4194304 | bytes 50332160 | tf_op jit(solution)/shard_map/while/body/eval_jaxpr/scatter-add | solution.py:27
  560.6 0.8 compare_and_fusion.5
  561.3 6.6 gather_fusion.1
  567.9 12.8 %convolution_multiply_fusion.5 = f32[128,128,256]{2,1,0:T(8,128)} fusion(f32[128]{0:T(128)S(1)} %get-tuple-element.394, bf16[128,128,256]{2,1,0:T(8,128)(2,1)} %gather_fusion.1, pred[128]{0:T(512)(128)(4,1)S(1)} %get-tuple-element.396, bf16[512,128,128]{1,2,0:T(8,128)(2,1)} %get-tuple-element.455, s32[]{:T(128)S(6)} %select_n.88), kind=kOutput, calls=%fused_computation.16.clone.1 | convolution fusion | flops 1082130432 | bytes 29360772 | tf_op jit(solution)/shard_map/while/body/eval_jaxpr/tba,tbf->taf/dot_general | solution.py:23
  580.7 0.8 compare_select_fusion.9
  581.5 38.3 %scatter_fusion.1 = f32[64,128,256]{2,1,0:T(8,128)} fusion(f32[64,128,256]{2,1,0:T(8,128)} %get-tuple-element.442, s32[128]{0:T(128)S(1)} %compare_select_fusion.9, f32[128,128,256]{2,1,0:T(8,128)} %convolution_multiply_fusion.5), kind=kCustom, calls=%fused_computation.3.clone.1 | custom fusion | flops 4194304 | bytes 50332160 | tf_op jit(solution)/shard_map/while/body/eval_jaxpr/scatter-add | solution.py:27
  619.8 0.8 compare_and_fusion.5
  620.5 6.6 gather_fusion.1
  627.1 12.8 %convolution_multiply_fusion.5 = f32[128,128,256]{2,1,0:T(8,128)} fusion(f32[128]{0:T(128)S(1)} %get-tuple-element.394, bf16[128,128,256]{2,1,0:T(8,128)(2,1)} %gather_fusion.1, pred[128]{0:T(512)(128)(4,1)S(1)} %get-tuple-element.396, bf16[512,128,128]{1,2,0:T(8,128)(2,1)} %get-tuple-element.455, s32[]{:T(128)S(6)} %select_n.88), kind=kOutput, calls=%fused_computation.16.clone.1 | convolution fusion | flops 1082130432 | bytes 29360772 | tf_op jit(solution)/shard_map/while/body/eval_jaxpr/tba,tbf->taf/dot_general | solution.py:23
  639.9 0.8 compare_select_fusion.9
  640.7 38.3 %scatter_fusion.1 = f32[64,128,256]{2,1,0:T(8,128)} fusion(f32[64,128,256]{2,1,0:T(8,128)} %get-tuple-element.442, s32[128]{0:T(128)S(1)} %compare_select_fusion.9, f32[128,128,256]{2,1,0:T(8,128)} %convolution_multiply_fusion.5), kind=kCustom, calls=%fused_computation.3.clone.1 | custom fusion | flops 4194304 | bytes 50332160 | tf_op jit(solution)/shard_map/while/body/eval_jaxpr/scatter-add | solution.py:27
  679.0 0.0 reduce-scatter.5.cloned.1.call-update
  679.0 0.0 all-reduce.2.cloned.1.call-start
  679.0 71.8 %reduce-scatter.5.cloned.1.call-done = f32[512,256]{1,0:T(8,128)} async-done(((f32[8192,256]{1,0:T(8,128)}), f32[512,256]{1,0:T(8,128)}) %reduce-scatter.5.cloned.1.call-update) | async-done | bytes 524304 | tf_op jit(solution)/shard_map/reduce_scatter | solution.py:65
  750.8 2.0 convolution_bitcast_fusion
  752.9 2.0 convolution_convert_fusion
  754.9 144.8 %all-reduce.2.cloned.1.call-done = f32[256,256]{0,1:T(8,128)} async-done(((f32[256,256]{0,1:T(8,128)}), f32[256,256]{0,1:T(8,128)}) %all-reduce.2.cloned.1.call-update) | async-done | bytes 262160 | tf_op jit(solution)/shard_map/psum | solution.py:72
  899.6 1.8 copy.12
  (18 shorter events, 0.1 us)
Async XLA Ops:
  7.2 1.0 copy-start
  7.2 44.2 %all-gather.3.cloned.1.call-start = ((), (), s32[]{:S(2)}) async-start(), calls=%async_computation.2 | async-start | bytes 4456448 | tf_op jit(solution)/shard_map/all_gather | solution.py:47
  10.0 371.3 %reduce-scatter.3.cloned.1.call-start = ((), (), s32[]{:S(2)}) async-start(), calls=%async_computation.3 | async-start | bytes 4718592 | tf_op jit(solution)/shard_map/reduce_scatter | solution.py:51
  53.8 327.5 %copy-start.3 = (bf16[512,256]{1,0:T(8,128)(2,1)S(1)}, bf16[512,256]{1,0:T(8,128)(2,1)}, u32[]{:S(2)}) copy-start(bf16[512,256]{1,0:T(8,128)(2,1)} %param.13) | copy-start | bytes 786436
  298.0 139.9 %all-gather.5.cloned.1.call-start = ((), (), s32[]{:S(2)}) async-start(), calls=%async_computation.4 | async-start | bytes 2359296 | tf_op jit(solution)/shard_map/all_gather | solution.py:54
  383.4 367.4 %reduce-scatter.5.cloned.1.call-start = ((), (), s32[]{:S(2)}) async-start(), calls=%async_computation.5 | async-start | bytes 8912896 | tf_op jit(solution)/shard_map/reduce_scatter | solution.py:65
  437.9 4.2 copy-start.1
  679.0 73.9 %copy-start.2 = (bf16[256,256]{1,0:T(8,128)(2,1)S(1)}, bf16[256,256]{1,0:T(8,128)(2,1)}, u32[]{:S(2)}) copy-start(bf16[256,256]{1,0:T(8,128)(2,1)} %param.12) | copy-start | bytes 393220
  679.0 220.6 %all-reduce.2.cloned.1.call-start = ((), (), s32[]{:S(2)}) async-start(), calls=%async_computation.6 | async-start | bytes 524288 | tf_op jit(solution)/shard_map/psum | solution.py:72
Sparse Core Ops, SparseCore 0:
  10.3 41.0 all-gather.2
  298.1 83.1 reduce-scatter.2
  384.2 53.6 all-gather.4
  679.1 71.6 reduce-scatter.4
  756.0 143.6 all-reduce.1
where the time goes:
time: 910 us; the launch traced here: 908 us
  waiting for transfers between devices  372 us (41%)
  other arithmetic  319 us (35%)
  matrix products  108 us (12%)
  local copies, waits for them, and re-layouts  93.1 us (10%)
  between operations  14.5 us (2%)
    scatter-add x8, other arithmetic, accumulate(): return summed.at[places].add(products)  305 us
    psum x1, waiting for transfers between devices, body(): grad_weight = lax.psum(local_weight, ('dom', 'rep'))  145 us
    dot_general x8, matrix products, accumulate(): jnp.einsum(pattern, block_values, picked, preferred_element_type=jnp.floa...  103 us
    reduce_scatter x1, waiting for transfers between devices, body(): lax.psum_scatter(partial_value, 'rep', scatter_dimension=0, tiled=True)  83.2 us
    reduce_scatter x1, waiting for transfers between devices, body(): lax.psum_scatter(back_partial, 'dom', scatter_dimension=0, tiled=True)  71.8 us
    gather x8, local copies, waits for them, and re-layouts, accumulate(): picked = jnp.take(source, picks, axis=0)  61.3 us
    all_gather x1, waiting for transfers between devices, body(): gathered = lax.all_gather(projected, 'dom', axis=0, tiled=True)  40.7 us
    all_gather x1, waiting for transfers between devices, body(): grad_block = lax.all_gather(grad_own, 'rep', axis=0, tiled=True)  31.9 us
  transfers between devices with their start and end apart: 5, of which 5 were waited for; matrix products, arithmetic and copies ran while one was open for 3% of the time, Pallas kernels for 0%

commit v1 on v0

--- a/solution.py
+++ b/solution.py
@@ -69,7 +69,7 @@
         jnp.bfloat16
     )
     local_weight = jnp.dot(node_features.T, grad_projected, preferred_element_type=jnp.float32)
-    grad_weight = lax.psum(local_weight, ("dom", "rep"))
+    grad_weight = jnp.sum(lax.all_gather(local_weight, ("dom", "rep")), axis=0)
     return (output, grad_features, grad_weight)
 
 

time: 910 us -> 1140 us (1.25)
  waiting for transfers between devices: 372 us -> 577 us
  local copies, waits for them, and re-layouts: 93.1 us -> 112 us
    all_gather x0 -> x1, waiting for transfers between devices: none -> 349 us  [body(): grad_weight = jnp.sum(lax.all_gather(local_weight, ('dom', 'rep')), axis=0)]
    psum x1 -> x0, waiting for transfers between devices: 145 us -> none  [body(): grad_weight = lax.psum(local_weight, ('dom', 'rep'))]
    unnamed x10 -> x11, local copies, waits for them, and re-layouts: 25.1 us -> 43.7 us
  transfers between devices with their start and end apart: 5 -> 5, of which waited for: 5 -> 5; matrix products, arithmetic and copies ran while one was open for 3% -> 2% of each run, Pallas kernels for 0% -> 0%
where the time goes in v1:
time: 1140 us
  waiting for transfers between devices  577 us (51%)
  other arithmetic  323 us (28%)
  local copies, waits for them, and re-layouts  112 us (10%)
  matrix products  108 us (9%)
  between operations  14.5 us (1%)
    all_gather x1, waiting for transfers between devices, body(): grad_weight = jnp.sum(lax.all_gather(local_weight, ('dom', 'rep')), axis=0)  349 us
    scatter-add x8, other arithmetic, accumulate(): return summed.at[places].add(products)  305 us
    dot_general x8, matrix products, accumulate(): jnp.einsum(pattern, block_values, picked, preferred_element_type=jnp.floa...  103 us
    reduce_scatter x1, waiting for transfers between devices, body(): lax.psum_scatter(partial_value, 'rep', scatter_dimension=0, tiled=True)  83.4 us
    reduce_scatter x1, waiting for transfers between devices, body(): lax.psum_scatter(back_partial, 'dom', scatter_dimension=0, tiled=True)  71.8 us
    gather x8, local copies, waits for them, and re-layouts, accumulate(): picked = jnp.take(source, picks, axis=0)  61.3 us
    unnamed x11, local copies, waits for them, and re-layouts  43.7 us
    all_gather x1, waiting for transfers between devices, body(): gathered = lax.all_gather(projected, 'dom', axis=0, tiled=True)  40.7 us
  transfers between devices with their start and end apart: 5, of which 5 were waited for; matrix products, arithmetic and copies ran while one was open for 2% of the time, Pallas kernels for 0%

profile of v1, /device:TPU:1, one launch (start us, length us, event | category | flops | bytes accessed | tf_op | source)
XLA Modules:
  0.0 1135.2 jit_solution(10089177089720881272)
XLA Ops:
  7.2 0.0 all-gather.5.cloned.1.call-start
  7.2 0.9 copy-done
  8.1 1.8 convolution_convert_fusion.1
  10.0 0.0 reduce-scatter.3.cloned.1.call-start
  10.7 40.7 %all-gather.5.cloned.1.call-done = bf16[8192,256]{1,0:T(8,128)(2,1)} async-done(((bf16[512,256]{1,0:T(8,128)(2,1)}), bf16[8192,256]{1,0:T(8,128)(2,1)}) %all-gather.5.cloned.1.call-update) | async-done | bytes 4194320 | tf_op jit(solution)/shard_map/all_gather | solution.py:47
  51.4 2.4 broadcast_in_dim.74
  53.8 244.2 %while.26 = (s32[]{:T(128)}, f32[32,128,256]{2,1,0:T(8,128)}, s32[512]{0:T(512)}, bf16[512,128,128]{2,1,0:T(8,128)(2,1)}, s32[512]{0:T(512)}, /*index=5*/bf16[64...) while((s32[]{:T(128)}, f32[32,128,256]{2,1,0:T(8,128)}, ...), condition=%wide.region_2.3_spmd, body=%wide.region_0.2_spmd.sunk | while | flops 1086327040 | bytes 96478248 | solution.py:30
  53.8 0.8 compare_select_fusion.8
  54.6 0.8 compare_and_fusion.4
  55.4 8.8 gather_fusion
  64.1 12.8 %convolution_multiply_fusion.4 = f32[128,128,256]{2,1,0:T(8,128)} fusion(f32[128]{0:T(128)S(1)} %get-tuple-element.391, bf16[128,128,256]{2,1,0:T(8,128)(2,1)} %gather_fusion, pred[128]{0:T(512)(128)(4,1)S(1)} %get-tuple-element.393, bf16[512,128,128]{2,1,0:T(8,128)(2,1)} %get-tuple-element.429, s32[]{:T(128)S(6)} %select_n.85), kind=kOutput, calls=%fused_computation.4.clone.1 | convolution fusion | flops 1082130432 | bytes 29360772 | tf_op jit(solution)/shard_map/while/body/eval_jaxpr/tab,tbf->taf/dot_general | solution.py:23
  76.9 38.1 %scatter_fusion = f32[32,128,256]{2,1,0:T(8,128)} fusion(f32[32,128,256]{2,1,0:T(8,128)} %get-tuple-element.416, s32[128]{0:T(128)S(1)} %compare_select_fusion.8, f32[128,128,256]{2,1,0:T(8,128)} %convolution_multiply_fusion.4), kind=kCustom, calls=%fused_computation.2.clone.1 | custom fusion | flops 4194304 | bytes 50332160 | tf_op jit(solution)/shard_map/while/body/eval_jaxpr/scatter-add | solution.py:27
  115.0 0.8 compare_select_fusion.8
  115.8 0.8 compare_and_fusion.4
  116.5 8.8 gather_fusion
  125.3 12.8 %convolution_multiply_fusion.4 = f32[128,128,256]{2,1,0:T(8,128)} fusion(f32[128]{0:T(128)S(1)} %get-tuple-element.391, bf16[128,128,256]{2,1,0:T(8,128)(2,1)} %gather_fusion, pred[128]{0:T(512)(128)(4,1)S(1)} %get-tuple-element.393, bf16[512,128,128]{2,1,0:T(8,128)(2,1)} %get-tuple-element.429, s32[]{:T(128)S(6)} %select_n.85), kind=kOutput, calls=%fused_computation.4.clone.1 | convolution fusion | flops 1082130432 | bytes 29360772 | tf_op jit(solution)/shard_map/while/body/eval_jaxpr/tab,tbf->taf/dot_general | solution.py:23
  138.1 38.1 %scatter_fusion = f32[32,128,256]{2,1,0:T(8,128)} fusion(f32[32,128,256]{2,1,0:T(8,128)} %get-tuple-element.416, s32[128]{0:T(128)S(1)} %compare_select_fusion.8, f32[128,128,256]{2,1,0:T(8,128)} %convolution_multiply_fusion.4), kind=kCustom, calls=%fused_computation.2.clone.1 | custom fusion | flops 4194304 | bytes 50332160 | tf_op jit(solution)/shard_map/while/body/eval_jaxpr/scatter-add | solution.py:27
  176.2 0.8 compare_select_fusion.8
  176.9 0.8 compare_and_fusion.4
  177.7 8.8 gather_fusion
  186.4 12.8 %convolution_multiply_fusion.4 = f32[128,128,256]{2,1,0:T(8,128)} fusion(f32[128]{0:T(128)S(1)} %get-tuple-element.391, bf16[128,128,256]{2,1,0:T(8,128)(2,1)} %gather_fusion, pred[128]{0:T(512)(128)(4,1)S(1)} %get-tuple-element.393, bf16[512,128,128]{2,1,0:T(8,128)(2,1)} %get-tuple-element.429, s32[]{:T(128)S(6)} %select_n.85), kind=kOutput, calls=%fused_computation.4.clone.1 | convolution fusion | flops 1082130432 | bytes 29360772 | tf_op jit(solution)/shard_map/while/body/eval_jaxpr/tab,tbf->taf/dot_general | solution.py:23
  199.3 37.7 %scatter_fusion = f32[32,128,256]{2,1,0:T(8,128)} fusion(f32[32,128,256]{2,1,0:T(8,128)} %get-tuple-element.416, s32[128]{0:T(128)S(1)} %compare_select_fusion.8, f32[128,128,256]{2,1,0:T(8,128)} %convolution_multiply_fusion.4), kind=kCustom, calls=%fused_computation.2.clone.1 | custom fusion | flops 4194304 | bytes 50332160 | tf_op jit(solution)/shard_map/while/body/eval_jaxpr/scatter-add | solution.py:27
  237.0 0.8 compare_select_fusion.8
  237.7 0.8 compare_and_fusion.4
  238.5 8.8 gather_fusion
  247.3 12.8 %convolution_multiply_fusion.4 = f32[128,128,256]{2,1,0:T(8,128)} fusion(f32[128]{0:T(128)S(1)} %get-tuple-element.391, bf16[128,128,256]{2,1,0:T(8,128)(2,1)} %gather_fusion, pred[128]{0:T(512)(128)(4,1)S(1)} %get-tuple-element.393, bf16[512,128,128]{2,1,0:T(8,128)(2,1)} %get-tuple-element.429, s32[]{:T(128)S(6)} %select_n.85), kind=kOutput, calls=%fused_computation.4.clone.1 | convolution fusion | flops 1082130432 | bytes 29360772 | tf_op jit(solution)/shard_map/while/body/eval_jaxpr/tab,tbf->taf/dot_general | solution.py:23
  260.1 37.9 %scatter_fusion = f32[32,128,256]{2,1,0:T(8,128)} fusion(f32[32,128,256]{2,1,0:T(8,128)} %get-tuple-element.416, s32[128]{0:T(128)S(1)} %compare_select_fusion.8, f32[128,128,256]{2,1,0:T(8,128)} %convolution_multiply_fusion.4), kind=kCustom, calls=%fused_computation.2.clone.1 | custom fusion | flops 4194304 | bytes 50332160 | tf_op jit(solution)/shard_map/while/body/eval_jaxpr/scatter-add | solution.py:27
  298.0 0.0 all-gather.7.cloned.1.call-start
  298.0 83.4 %reduce-scatter.3.cloned.1.call-done = f32[512,256]{1,0:T(8,128)} async-done(((f32[4096,256]{1,0:T(8,128)}), f32[512,256]{1,0:T(8,128)}) %reduce-scatter.3.cloned.1.call-update) | async-done | bytes 524304 | tf_op jit(solution)/shard_map/reduce_scatter | solution.py:51
  381.5 2.1 multiply_convert_fusion
  383.5 0.0 all-gather.7.cloned.1.call-update
  383.6 0.2 reduce-scatter.5.cloned.1.call-start
  383.8 22.4 %copy.12 = bf16[1,1,512,128,128]{3,4,2,1,0:T(8,128)(2,1)} copy(bf16[1,1,512,128,128]{4,3,2,1,0:T(8,128)(2,1)} %bitcast.26) | data formatting | bytes 33554432 | tf_op args[5]
  406.2 31.8 %all-gather.7.cloned.1.call-done = bf16[4096,256]{1,0:T(8,128)(2,1)} async-done(((bf16[512,256]{1,0:T(8,128)(2,1)}), bf16[4096,256]{1,0:T(8,128)(2,1)}) %all-gather.7.cloned.1.call-update) | async-done | bytes 2097168 | tf_op jit(solution)/shard_map/all_gather | solution.py:54
  437.9 4.2 broadcast_in_dim.75
  442.2 236.8 %while.27 = (s32[]{:T(128)}, f32[64,128,256]{2,1,0:T(8,128)}, s32[512]{0:T(512)}, bf16[512,128,128]{1,2,0:T(8,128)(2,1)}, s32[512]{0:T(512)}, /*index=5*/bf16[32...) while((s32[]{:T(128)}, f32[64,128,256]{2,1,0:T(8,128)}, ...), condition=%wide.region_6.7_spmd, body=%wide.region_4.6_spmd.sunk | while | flops 1086327040 | bytes 96478248 | solution.py:30
  442.2 0.8 compare_select_fusion.9
  442.9 0.8 compare_and_fusion.5
  443.7 6.6 gather_fusion.1
  450.3 12.8 %convolution_multiply_fusion.5 = f32[128,128,256]{2,1,0:T(8,128)} fusion(f32[128]{0:T(128)S(1)} %get-tuple-element.401, bf16[128,128,256]{2,1,0:T(8,128)(2,1)} %gather_fusion.1, pred[128]{0:T(512)(128)(4,1)S(1)} %get-tuple-element.403, bf16[512,128,128]{1,2,0:T(8,128)(2,1)} %get-tuple-element.462, s32[]{:T(128)S(6)} %select_n.88), kind=kOutput, calls=%fused_computation.16.clone.1 | convolution fusion | flops 1082130432 | bytes 29360772 | tf_op jit(solution)/shard_map/while/body/eval_jaxpr/tba,tbf->taf/dot_general | solution.py:23
  463.1 38.5 %scatter_fusion.1 = f32[64,128,256]{2,1,0:T(8,128)} fusion(f32[64,128,256]{2,1,0:T(8,128)} %get-tuple-element.449, s32[128]{0:T(128)S(1)} %compare_select_fusion.9, f32[128,128,256]{2,1,0:T(8,128)} %convolution_multiply_fusion.5), kind=kCustom, calls=%fused_computation.3.clone.1 | custom fusion | flops 4194304 | bytes 50332160 | tf_op jit(solution)/shard_map/while/body/eval_jaxpr/scatter-add | solution.py:27
  501.6 0.8 compare_select_fusion.9
  502.3 0.8 compare_and_fusion.5
  503.1 6.6 gather_fusion.1
  509.7 12.8 %convolution_multiply_fusion.5 = f32[128,128,256]{2,1,0:T(8,128)} fusion(f32[128]{0:T(128)S(1)} %get-tuple-element.401, bf16[128,128,256]{2,1,0:T(8,128)(2,1)} %gather_fusion.1, pred[128]{0:T(512)(128)(4,1)S(1)} %get-tuple-element.403, bf16[512,128,128]{1,2,0:T(8,128)(2,1)} %get-tuple-element.462, s32[]{:T(128)S(6)} %select_n.88), kind=kOutput, calls=%fused_computation.16.clone.1 | convolution fusion | flops 1082130432 | bytes 29360772 | tf_op jit(solution)/shard_map/while/body/eval_jaxpr/tba,tbf->taf/dot_general | solution.py:23
  522.5 38.1 %scatter_fusion.1 = f32[64,128,256]{2,1,0:T(8,128)} fusion(f32[64,128,256]{2,1,0:T(8,128)} %get-tuple-element.449, s32[128]{0:T(128)S(1)} %compare_select_fusion.9, f32[128,128,256]{2,1,0:T(8,128)} %convolution_multiply_fusion.5), kind=kCustom, calls=%fused_computation.3.clone.1 | custom fusion | flops 4194304 | bytes 50332160 | tf_op jit(solution)/shard_map/while/body/eval_jaxpr/scatter-add | solution.py:27
  560.6 0.8 compare_select_fusion.9
  561.3 0.8 compare_and_fusion.5
  562.1 6.6 gather_fusion.1
  568.7 12.8 %convolution_multiply_fusion.5 = f32[128,128,256]{2,1,0:T(8,128)} fusion(f32[128]{0:T(128)S(1)} %get-tuple-element.401, bf16[128,128,256]{2,1,0:T(8,128)(2,1)} %gather_fusion.1, pred[128]{0:T(512)(128)(4,1)S(1)} %get-tuple-element.403, bf16[512,128,128]{1,2,0:T(8,128)(2,1)} %get-tuple-element.462, s32[]{:T(128)S(6)} %select_n.88), kind=kOutput, calls=%fused_computation.16.clone.1 | convolution fusion | flops 1082130432 | bytes 29360772 | tf_op jit(solution)/shard_map/while/body/eval_jaxpr/tba,tbf->taf/dot_general | solution.py:23
  581.5 38.3 %scatter_fusion.1 = f32[64,128,256]{2,1,0:T(8,128)} fusion(f32[64,128,256]{2,1,0:T(8,128)} %get-tuple-element.449, s32[128]{0:T(128)S(1)} %compare_select_fusion.9, f32[128,128,256]{2,1,0:T(8,128)} %convolution_multiply_fusion.5), kind=kCustom, calls=%fused_computation.3.clone.1 | custom fusion | flops 4194304 | bytes 50332160 | tf_op jit(solution)/shard_map/while/body/eval_jaxpr/scatter-add | solution.py:27
  619.8 0.8 compare_select_fusion.9
  620.6 0.8 compare_and_fusion.5
  621.3 6.6 gather_fusion.1
  627.9 12.8 %convolution_multiply_fusion.5 = f32[128,128,256]{2,1,0:T(8,128)} fusion(f32[128]{0:T(128)S(1)} %get-tuple-element.401, bf16[128,128,256]{2,1,0:T(8,128)(2,1)} %gather_fusion.1, pred[128]{0:T(512)(128)(4,1)S(1)} %get-tuple-element.403, bf16[512,128,128]{1,2,0:T(8,128)(2,1)} %get-tuple-element.462, s32[]{:T(128)S(6)} %select_n.88), kind=kOutput, calls=%fused_computation.16.clone.1 | convolution fusion | flops 1082130432 | bytes 29360772 | tf_op jit(solution)/shard_map/while/body/eval_jaxpr/tba,tbf->taf/dot_general | solution.py:23
  640.7 38.3 %scatter_fusion.1 = f32[64,128,256]{2,1,0:T(8,128)} fusion(f32[64,128,256]{2,1,0:T(8,128)} %get-tuple-element.449, s32[128]{0:T(128)S(1)} %compare_select_fusion.9, f32[128,128,256]{2,1,0:T(8,128)} %convolution_multiply_fusion.5), kind=kCustom, calls=%fused_computation.3.clone.1 | custom fusion | flops 4194304 | bytes 50332160 | tf_op jit(solution)/shard_map/while/body/eval_jaxpr/scatter-add | solution.py:27
  679.0 0.0 all-gather.9.cloned.1.call-start
  679.1 71.8 %reduce-scatter.5.cloned.1.call-done = f32[512,256]{1,0:T(8,128)} async-done(((f32[8192,256]{1,0:T(8,128)}), f32[512,256]{1,0:T(8,128)}) %reduce-scatter.5.cloned.1.call-update) | async-done | bytes 524304 | tf_op jit(solution)/shard_map/reduce_scatter | solution.py:65
  750.9 2.0 convolution_bitcast_fusion
  753.0 2.0 convolution_convert_fusion
  755.0 349.1 %all-gather.9.cloned.1.call-done = f32[32768,256]{0,1:T(8,128)} async-done(((f32[256,256]{0,1:T(8,128)}), f32[32768,256]{0,1:T(8,128)}) %all-gather.9.cloned.1.call-update) | async-done | bytes 33554448 | tf_op jit(solution)/shard_map/all_gather | solution.py:72
  1104.1 19.6 %copy.16 = f32[32,8,128,256]{3,2,1,0:T(8,128)S(1)} copy(f32[32,8,128,256]{3,1,2,0:T(8,128)} %bitcast.28) | data formatting | bytes 67108864
  1123.7 4.1 bitcast_reduce_fusion
  1127.8 0.8 copy.14
  (20 shorter events, 0.1 us)
Async XLA Ops:
  7.2 1.0 copy-start
  7.2 44.2 %all-gather.5.cloned.1.call-start = ((), (), s32[]{:S(2)}) async-start(), calls=%async_computation.2 | async-start | bytes 4456448 | tf_op jit(solution)/shard_map/all_gather | solution.py:47
  10.0 371.5 %reduce-scatter.3.cloned.1.call-start = ((), (), s32[]{:S(2)}) async-start(), calls=%async_computation.3 | async-start | bytes 4718592 | tf_op jit(solution)/shard_map/reduce_scatter | solution.py:51
  53.8 327.7 %copy-start.3 = (bf16[512,256]{1,0:T(8,128)(2,1)S(1)}, bf16[512,256]{1,0:T(8,128)(2,1)}, u32[]{:S(2)}) copy-start(bf16[512,256]{1,0:T(8,128)(2,1)} %param.13) | copy-start | bytes 786436
  298.0 139.9 %all-gather.7.cloned.1.call-start = ((), (), s32[]{:S(2)}) async-start(), calls=%async_computation.4 | async-start | bytes 2359296 | tf_op jit(solution)/shard_map/all_gather | solution.py:54
  383.6 367.4 %reduce-scatter.5.cloned.1.call-start = ((), (), s32[]{:S(2)}) async-start(), calls=%async_computation.5 | async-start | bytes 8912896 | tf_op jit(solution)/shard_map/reduce_scatter | solution.py:65
  437.9 4.2 copy-start.1
  679.0 74.0 %copy-start.2 = (bf16[256,256]{1,0:T(8,128)(2,1)S(1)}, bf16[256,256]{1,0:T(8,128)(2,1)}, u32[]{:S(2)}) copy-start(bf16[256,256]{1,0:T(8,128)(2,1)} %param.12) | copy-start | bytes 393220
  679.0 425.1 %all-gather.9.cloned.1.call-start = ((), (), s32[]{:S(2)}) async-start(), calls=%async_computation.6 | async-start | bytes 33816576 | tf_op jit(solution)/shard_map/all_gather | solution.py:72
Sparse Core Ops, SparseCore 0:
  10.3 41.0 all-gather.4
  298.1 83.2 reduce-scatter.2
  384.4 53.5 all-gather.6
  679.1 71.7 reduce-scatter.4
  753.1 350.9 all-gather.8
